TPU v7x, 32 devices: a whole 2x2x4 slice. The times are simulated.
32 devices in a mesh: dp: 4 (over y, core), tensor: 8 (over z, x).
Axes of the slice: x: 2, y: 2, z: 4, core: 2. Of those that a mesh axis runs over, the one named last changes fastest.
Arguments:
- tokens: bfloat16 [8192, 2048], P(('dp', 'tensor')), may hold values from -6 to 6
- gain_one: float32 [2048], replicated, may hold values from 0.5 to 1.5
- w_query: bfloat16 [2048, 256], P(None, 'tensor'), may hold values from -0.125 to 0.125
- w_key: bfloat16 [2048, 256], P(None, 'tensor'), may hold values from -0.125 to 0.125
- w_value: bfloat16 [2048, 2048], P(None, 'tensor'), may hold values from -0.125 to 0.125
- w_out: bfloat16 [2048, 2048], P('tensor'), may hold values from -0.5 to 0.5
- gain_two: float32 [2048], replicated, may hold values from 0.5 to 1.5
- w_gate: bfloat16 [2048, 5632], P(None, 'tensor'), may hold values from -0.125 to 0.125
- w_up: bfloat16 [2048, 5632], P(None, 'tensor'), may hold values from -0.125 to 0.125
- w_down: bfloat16 [5632, 2048], P('tensor'), may hold values from -0.078125 to 0.078125
- doc_ids: int32 [4, 2048], P('dp'), may hold values from 0 to 7, never falling along the last dimension, each value on 1 to 1024 neighbouring positions
- cotangent: bfloat16 [8192, 2048], P(('dp', 'tensor')), may hold values from -6 to 6
Outputs:
- block_out: bfloat16 [8192, 2048], P(('dp', 'tensor'))
- grad_tokens: float32 [8192, 2048], P(('dp', 'tensor'))
- grad_gain_one: float32 [2048], replicated
- grad_query: float32 [2048, 256], P(None, 'tensor')
- grad_key: float32 [2048, 256], P(None, 'tensor')
- grad_value: float32 [2048, 2048], P(None, 'tensor')
- grad_out_proj: float32 [2048, 2048], P('tensor')
- grad_gain_two: float32 [2048], replicated
- grad_gate: float32 [2048, 5632], P(None, 'tensor')
- grad_up: float32 [2048, 5632], P(None, 'tensor')
- grad_down: float32 [5632, 2048], P('tensor')
Inputs may be any that keep to these rules, and one draw needn't show every extreme that they name: Each row of doc_ids never falls along the row; each of the 8 documents of a group has 1 to 1024 tokens, and one has exactly 1024.
All inputs are finite; a program needn't handle non-finite values.
Results may differ from a plain program's by a relative error of at most 0.02.
Values may be sent and summed in bfloat16 or wider, within the bound.
No kernel may reach another device: no remote copies, remote signals or barrier semaphores. Data moves between devices by JAX's collectives and lax.ppermute only.
A program may use at most 256 MiB of HBM per device.

v0:
```python
import jax
import jax.numpy as jnp
from jax import lax
from jax.sharding import PartitionSpec as P

FEAT = 16
HEAD_V = 128
EPS = 1e-05


def norm_rows(values, gain_vec):
    row_scale = lax.rsqrt(jnp.mean(values * values, axis=-1, keepdims=True) + EPS)
    normed = values * row_scale
    return (normed, row_scale, (normed * gain_vec).astype(jnp.bfloat16))


def norm_back(grad_normed, normed, row_scale, gain_vec):
    weighted = grad_normed * gain_vec
    inner_mean = jnp.mean(weighted * normed, axis=-1, keepdims=True)
    return (row_scale * (weighted - normed * inner_mean), jnp.sum(grad_normed * normed, axis=0))


def contract_rows(left_mat, right_mat):
    return lax.dot_general(
        left_mat, right_mat, (((0,), (0,)), ((), ())), preferred_element_type=jnp.float32
    )


def times_transposed(left_mat, right_mat):
    return lax.dot_general(
        left_mat, right_mat, (((1,), (1,)), ((), ())), preferred_element_type=jnp.float32
    )


def block_kernel(query_rows, key_row_block, doc_row, row_start, block_rows):
    row_end_index = row_start + block_rows
    query_portion = query_rows[row_start:row_end_index]
    score_matrix = (
        jnp.einsum(
            "gsn,jsn->sgj",
            query_portion,
            key_row_block[:row_end_index],
            preferred_element_type=jnp.float32,
        )
        * 0.25
    )
    query_index = row_start + jnp.arange(block_rows)
    key_index = jnp.arange(row_end_index)
    allowed = (doc_row[row_start:row_end_index, None] == doc_row[None, :row_end_index]) & (
        query_index[:, None] >= key_index[None, :]
    )
    kernel = jnp.where(allowed[None], 1.0 + score_matrix + 0.5 * score_matrix * score_matrix, 0.0)
    return (score_matrix, allowed, kernel)


def attention_forward(query_rows, key_row_block, value_rows, doc_row, block_rows):
    group_rows = query_rows.shape[0]
    outputs = []
    denoms = []
    for row_start in range(0, group_rows, block_rows):
        row_end_index = row_start + block_rows
        score_matrix, allowed, kernel = block_kernel(
            query_rows, key_row_block, doc_row, row_start, block_rows
        )
        denominator = jnp.sum(kernel, axis=-1)
        numerator = jnp.einsum(
            "hqk,khd->qhd",
            kernel.astype(jnp.bfloat16),
            value_rows[:row_end_index],
            preferred_element_type=jnp.float32,
        )
        outputs.append((numerator / denominator.T[:, :, None]).astype(jnp.bfloat16))
        denoms.append(denominator)
    return (jnp.concatenate(outputs, axis=0), jnp.concatenate(denoms, axis=1))


def attention_backward(
    query_rows, key_row_block, value_rows, doc_row, denoms, grad_mixed, block_rows
):
    group_rows = query_rows.shape[0]
    grad_queries = []
    grad_keys = jnp.zeros(key_row_block.shape, jnp.float32)
    grad_values = jnp.zeros(value_rows.shape, jnp.float32)
    for row_start in range(0, group_rows, block_rows):
        row_end_index = row_start + block_rows
        score_matrix, allowed, kernel = block_kernel(
            query_rows, key_row_block, doc_row, row_start, block_rows
        )
        kernel_low = kernel.astype(jnp.bfloat16)
        denominator = denoms[:, row_start:row_end_index]
        numerator = jnp.einsum(
            "hqk,khd->qhd",
            kernel_low,
            value_rows[:row_end_index],
            preferred_element_type=jnp.float32,
        )
        grad_output = grad_mixed[row_start:row_end_index].astype(jnp.float32)
        grad_numer = (grad_output / denominator.T[:, :, None]).astype(jnp.bfloat16)
        grad_denom = -jnp.sum(grad_output * numerator, axis=-1).T / (denominator * denominator)
        grad_kernel = (
            jnp.einsum(
                "qhd,khd->hqk",
                grad_numer,
                value_rows[:row_end_index],
                preferred_element_type=jnp.float32,
            )
            + grad_denom[:, :, None]
        )
        score_gradients = jnp.where(allowed[None], grad_kernel * (1.0 + score_matrix), 0.0).astype(
            jnp.bfloat16
        )
        grad_queries.append(
            jnp.einsum(
                "zxu,uzc->xzc",
                score_gradients,
                key_row_block[:row_end_index],
                preferred_element_type=jnp.float32,
            )
            * 0.25
        )
        grad_keys = grad_keys.at[:row_end_index].add(
            jnp.einsum(
                "ari,ran->ian",
                score_gradients,
                query_rows[row_start:row_end_index],
                preferred_element_type=jnp.float32,
            )
            * 0.25
        )
        grad_values = grad_values.at[:row_end_index].add(
            jnp.einsum("hqk,qhd->khd", kernel_low, grad_numer, preferred_element_type=jnp.float32)
        )
    grad_query_rows = jnp.concatenate(grad_queries, axis=0).astype(jnp.bfloat16)
    return (grad_query_rows, grad_keys.astype(jnp.bfloat16), grad_values.astype(jnp.bfloat16))


def body(
    tokens,
    gain_one,
    w_query,
    w_key,
    w_value,
    w_out,
    gain_two,
    w_gate,
    w_up,
    w_down,
    doc_ids,
    cotangent,
):
    heads_here = w_query.shape[1] // FEAT
    doc_row = doc_ids[0]
    inputs = tokens.astype(jnp.float32)
    normed_one, scale_one, low_one = norm_rows(inputs, gain_one)
    gathered_one = lax.all_gather(low_one, "tensor", axis=0, tiled=True)
    group_rows = gathered_one.shape[0]
    block_rows = min(512, group_rows)
    query_flat = jnp.dot(gathered_one, w_query, preferred_element_type=jnp.float32).astype(
        jnp.bfloat16
    )
    key_flat = jnp.dot(gathered_one, w_key, preferred_element_type=jnp.float32).astype(jnp.bfloat16)
    value_flat = jnp.dot(gathered_one, w_value, preferred_element_type=jnp.float32).astype(
        jnp.bfloat16
    )
    query_rows = query_flat.reshape(group_rows, heads_here, FEAT)
    key_row_block = key_flat.reshape(group_rows, heads_here, FEAT)
    value_rows = value_flat.reshape(group_rows, heads_here, HEAD_V)
    mixed_blocks, denoms = attention_forward(
        query_rows, key_row_block, value_rows, doc_row, block_rows
    )
    mixed_heads = mixed_blocks.reshape(group_rows, heads_here * HEAD_V)
    part_rows = mixed_heads
    attn_out = lax.psum_scatter(
        jnp.dot(part_rows, w_out, preferred_element_type=jnp.float32),
        "tensor",
        scatter_dimension=0,
        tiled=True,
    )
    residual = inputs + attn_out
    normed_two, scale_two, low_two = norm_rows(residual, gain_two)
    gathered_two = lax.all_gather(low_two, "tensor", axis=0, tiled=True)
    gate_pre = jnp.dot(gathered_two, w_gate, preferred_element_type=jnp.float32)
    upward = jnp.dot(gathered_two, w_up, preferred_element_type=jnp.float32)
    sigmoid_gate = jax.nn.sigmoid(gate_pre)
    hidden = (gate_pre * sigmoid_gate * upward).astype(jnp.bfloat16)
    part_rows = hidden
    ffn_out = lax.psum_scatter(
        jnp.dot(part_rows, w_down, preferred_element_type=jnp.float32).astype(jnp.bfloat16),
        "tensor",
        scatter_dimension=0,
        tiled=True,
    ).astype(jnp.float32)
    block_out = (residual + ffn_out).astype(jnp.bfloat16)
    grad_rows = lax.all_gather(cotangent, "tensor", axis=0, tiled=True)
    grad_down_w = contract_rows(hidden, grad_rows)
    grad_hidden = times_transposed(grad_rows, w_down)
    slope_gate = sigmoid_gate * (1.0 + gate_pre * (1.0 - sigmoid_gate))
    grad_gate_act = (grad_hidden * upward * slope_gate).astype(jnp.bfloat16)
    grad_upward = (grad_hidden * (gate_pre * sigmoid_gate)).astype(jnp.bfloat16)
    grad_gate_w = contract_rows(gathered_two, grad_gate_act)
    grad_up_w = contract_rows(gathered_two, grad_upward)
    grad_normed_two = lax.psum_scatter(
        (times_transposed(grad_gate_act, w_gate) + times_transposed(grad_upward, w_up)).astype(
            jnp.bfloat16
        ),
        "tensor",
        scatter_dimension=0,
        tiled=True,
    ).astype(jnp.float32)
    grad_resid_norm, gain_two_part = norm_back(grad_normed_two, normed_two, scale_two, gain_two)
    grad_resid = cotangent.astype(jnp.float32) + grad_resid_norm
    grad_attn = grad_resid.astype(jnp.bfloat16)
    grad_attn_rows = lax.all_gather(grad_attn, "tensor", axis=0, tiled=True)
    grad_mixed = times_transposed(grad_attn_rows, w_out).astype(jnp.bfloat16)
    grad_out_w = contract_rows(mixed_heads, grad_attn_rows)
    grad_query_rows, grad_key_rows, grad_value_rows = attention_backward(
        query_rows,
        key_row_block,
        value_rows,
        doc_row,
        denoms,
        grad_mixed.reshape(group_rows, heads_here, HEAD_V),
        block_rows,
    )
    grad_query_flat = grad_query_rows.reshape(group_rows, heads_here * FEAT)
    grad_key_flat = grad_key_rows.reshape(group_rows, heads_here * FEAT)
    grad_value_flat = grad_value_rows.reshape(group_rows, heads_here * HEAD_V)
    grad_query_w = contract_rows(gathered_one, grad_query_flat)
    grad_key_w = contract_rows(gathered_one, grad_key_flat)
    grad_value_w = contract_rows(gathered_one, grad_value_flat)
    grad_normed_one = lax.psum_scatter(
        (
            times_transposed(grad_query_flat, w_query)
            + times_transposed(grad_key_flat, w_key)
            + times_transposed(grad_value_flat, w_value)
        ).astype(jnp.bfloat16),
        "tensor",
        scatter_dimension=0,
        tiled=True,
    ).astype(jnp.float32)
    grad_input_norm, gain_one_part = norm_back(grad_normed_one, normed_one, scale_one, gain_one)
    grad_tokens = grad_resid + grad_input_norm
    gain_grads = lax.psum((gain_one_part, gain_two_part), ("dp", "tensor"))
    weight_grads = (
        lax.psum(grad_query_w.astype(jnp.bfloat16), "dp").astype(jnp.float32),
        lax.psum(grad_key_w.astype(jnp.bfloat16), "dp").astype(jnp.float32),
        lax.psum(grad_value_w.astype(jnp.bfloat16), "dp").astype(jnp.float32),
        lax.psum(grad_out_w.astype(jnp.bfloat16), "dp").astype(jnp.float32),
        lax.psum(grad_gate_w.astype(jnp.bfloat16), "dp").astype(jnp.float32),
        lax.psum(grad_up_w.astype(jnp.bfloat16), "dp").astype(jnp.float32),
        lax.psum(grad_down_w.astype(jnp.bfloat16), "dp").astype(jnp.float32),
    )
    return (
        block_out,
        grad_tokens,
        gain_grads[0],
        weight_grads[0],
        weight_grads[1],
        weight_grads[2],
        weight_grads[3],
        gain_grads[1],
        weight_grads[4],
        weight_grads[5],
        weight_grads[6],
    )


def solution(mesh):
    in_specs = (
        P(("dp", "tensor"), None),
        P(),
        P(None, "tensor"),
        P(None, "tensor"),
        P(None, "tensor"),
        P("tensor", None),
        P(),
        P(None, "tensor"),
        P(None, "tensor"),
        P("tensor", None),
        P("dp", None),
        P(("dp", "tensor"), None),
    )
    out_specs = (
        P(("dp", "tensor"), None),
        P(("dp", "tensor"), None),
        P(),
        P(None, "tensor"),
        P(None, "tensor"),
        P(None, "tensor"),
        P("tensor", None),
        P(),
        P(None, "tensor"),
        P(None, "tensor"),
        P("tensor", None),
    )
    return jax.shard_map(body, mesh=mesh, in_specs=in_specs, out_specs=out_specs, check_vma=False)
```

profile of v0, /device:TPU:0, one launch (start us, length us, event | category | flops | bytes accessed | tf_op | source)
XLA Modules:
  0.0 1586.6 jit_solution(5318080155431390041)
XLA Ops:
  17.0 122.2 %all-gather.5.cloned.1.call-done = bf16[2048,2048]{1,0:T(8,128)(2,1)} async-done(((bf16[256,2048]{1,0:T(8,128)(2,1)}), bf16[2048,2048]{1,0:T(8,128)(2,1)}) %all-gather.5.cloned.1.call-update) | async-done | bytes 8388624 | tf_op jit(solution)/shard_map/all_gather | solution.py:155
  170.0 8.2 fusion.81
  178.7 280.7 %reduce-scatter.5.cloned.1.call-done = f32[256,2048]{1,0:T(8,128)} async-done(((f32[2048,2048]{1,0:T(8,128)}), f32[256,2048]{1,0:T(8,128)}) %reduce-scatter.5.cloned.1.call-update) | async-done | bytes 2097168 | tf_op jit(solution)/shard_map/reduce_scatter | solution.py:173
  464.8 123.5 %all-gather.7.cloned.1.call-done = bf16[2048,2048]{1,0:T(8,128)(2,1)} async-done(((bf16[256,2048]{1,0:T(8,128)(2,1)}), bf16[2048,2048]{1,0:T(8,128)(2,1)}) %all-gather.7.cloned.1.call-update) | async-done | bytes 8388624 | tf_op jit(solution)/shard_map/all_gather | solution.py:181
  588.3 11.2 fusion.83
  599.5 8.0 fusion.82
  607.5 106.2 %all-gather.9.cloned.1.call-done = bf16[2048,2048]{1,0:T(8,128)(2,1)} async-done(((bf16[256,2048]{1,0:T(8,128)(2,1)}), bf16[2048,2048]{1,0:T(8,128)(2,1)}) %all-gather.9.cloned.1.call-update) | async-done | bytes 8388624 | tf_op jit(solution)/shard_map/all_gather | solution.py:194
  713.7 14.6 multiply_convert_fusion
  728.3 10.5 fusion.84
  738.8 12.6 add_convert_fusion.1
  751.4 147.3 %reduce-scatter.9.cloned.1.call-done = bf16[256,2048]{1,0:T(8,128)(2,1)} async-done(((bf16[2048,2048]{1,0:T(8,128)(2,1)}), bf16[256,2048]{1,0:T(8,128)(2,1)}) %reduce-scatter.9.cloned.1.call-update) | async-done | bytes 1048592 | tf_op jit(solution)/shard_map/reduce_scatter | solution.py:202
  906.1 10.9 convolution_convert_fusion.1
  917.0 10.9 convolution_convert_fusion.2
  928.0 7.8 convolution_convert_fusion.3
  935.8 94.3 %all-gather.11.cloned.1.call-done = bf16[2048,2048]{1,0:T(8,128)(2,1)} async-done(((bf16[256,2048]{1,0:T(8,128)(2,1)}), bf16[2048,2048]{1,0:T(8,128)(2,1)}) %all-gather.11.cloned.1.call-update) | async-done | bytes 8388624 | tf_op jit(solution)/shard_map/all_gather | solution.py:213
  1030.1 6.1 convolution_convert_fusion.6
  1072.8 8.6 fusion.58
  1081.4 8.1 fusion.85
  1089.5 15.9 add_convert_fusion
  1105.4 11.0 convolution_convert_fusion
  1116.5 151.1 %all-reduce.6.cloned.1.call-done = (bf16[2048,32]{0,1:T(8,128)(2,1)}, bf16[2048,32]{0,1:T(8,128)(2,1)}, bf16[2048,256]{1,0:T(8,128)(2,1)}, bf16[256,2048]{1,0:T(...) async-done(((bf16[2048,32]{0,1:T(8,128)(2,1)}, bf16[2048,32]{0,1:T(8,128)(2,1)}, bf16[2048,256]{1,0:T(8,128)(2,1)}, ...) | async-done | bytes 11010064 | tf_op jit(solution)/shard_map/psum | solution.py:245
  1285.3 135.2 %reduce-scatter.11.cloned.1.call-done = bf16[256,2048]{1,0:T(8,128)(2,1)} async-done(((bf16[2048,2048]{1,0:T(8,128)(2,1)}), bf16[256,2048]{1,0:T(8,128)(2,1)}) %reduce-scatter.11.cloned.1.call-update) | async-done | bytes 1048592 | tf_op jit(solution)/shard_map/reduce_scatter | solution.py:231
  1422.9 42.8 %all-reduce.2 = (f32[2048]{0:T(1024)}, f32[2048]{0:T(1024)}) all-reduce(f32[2048]{0:T(1024)S(1)} %get-tuple-element.125, f32[2048]{0:T(1024)S(1)} %copy-done.56), channel_id=1, replica_groups=mesh['dp'=4,'tensor'=8] {'dp','tensor'}, use_global_device_ids=true, to_apply=%region_17.18 | all-reduce | flops 4096 | bytes 32768 | tf_op jit(solution)/shard_map/psum | solution.py:243
  1465.7 107.9 %reduce-scatter.7.cloned.1.call-done = bf16[256,2048]{1,0:T(8,128)(2,1)} async-done(((bf16[2048,2048]{1,0:T(8,128)(2,1)}), bf16[256,2048]{1,0:T(8,128)(2,1)}) %reduce-scatter.7.cloned.1.call-update) | async-done | bytes 1048592 | tf_op jit(solution)/shard_map/reduce_scatter | solution.py:187
  (288 shorter events, 115.4 us)
Async XLA Ops:
  7.2 706.5 %copy-start = (bf16[704,2048]{1,0:T(8,128)(2,1)S(1)}, bf16[704,2048]{1,0:T(8,128)(2,1)}, u32[]{:S(2)}) copy-start(bf16[704,2048]{1,0:T(8,128)(2,1)} %param.41) | copy-start | bytes 8650756
  7.2 132.1 %copy-start.25 = (bf16[2048,32]{0,1:T(8,128)(2,1)S(1)}, bf16[2048,32]{0,1:T(8,128)(2,1)}, u32[]{:S(2)}) copy-start(bf16[2048,32]{0,1:T(8,128)(2,1)} %param.35) | copy-start | bytes 393220
  7.2 132.0 %all-gather.5.cloned.1.call-start = ((), (), s32[]{:S(2)}) async-start(), calls=%async_computation.4 | async-start | bytes 9437184 | tf_op jit(solution)/shard_map/all_gather | solution.py:155
  11.5 447.9 %reduce-scatter.5.cloned.1.call-start = ((), (), s32[]{:S(2)}) async-start(), calls=%async_computation.5 | async-start | bytes 18874368 | tf_op jit(solution)/shard_map/reduce_scatter | solution.py:173
  13.1 142.0 %copy-start.27 = (pred[512,1024]{1,0:T(8,128)(4,1)}, pred[512,1024]{1,0:T(8,128)(4,1)S(1)}, u32[]{:S(2)}) copy-start(pred[512,1024]{1,0:T(8,128)(4,1)S(1)} %fusion.36) | copy-start | bytes 1572868
  145.4 17.2 %copy-start.11 = (bf16[2048,32]{0,1:T(8,128)(2,1)}, bf16[2048,32]{0,1:T(8,128)(2,1)S(1)}, u32[]{:S(2)}) copy-start(bf16[2048,32]{0,1:T(8,128)(2,1)S(1)} %convolution_convert_fusion.10) | copy-start | bytes 393220
  147.9 17.8 %copy-start.9 = (bf16[2048,256]{0,1:T(8,128)(2,1)}, bf16[2048,256]{0,1:T(8,128)(2,1)S(1)}, u32[]{:S(2)}) copy-start(bf16[2048,256]{0,1:T(8,128)(2,1)S(1)} %convolution_convert_fusion.7) | copy-start | bytes 3145732
  178.3 284.7 %copy-start.44 = (f32[2048]{0:T(1024)S(1)}, f32[2048]{0:T(1024)}, u32[]{:S(2)}) copy-start(f32[2048]{0:T(1024)} %param.38) | copy-start | bytes 24580
  178.3 410.0 %all-gather.7.cloned.1.call-start = ((), (), s32[]{:S(2)}) async-start(), calls=%async_computation.6 | async-start | bytes 9437184 | tf_op jit(solution)/shard_map/all_gather | solution.py:181
  461.6 440.5 %copy-start.57 = (f32[256]{0:T(256)}, f32[256]{0:T(256)S(1)}, u32[]{:S(2)}) copy-start(f32[256]{0:T(256)S(1)} %add_rsqrt_fusion) | copy-start | bytes 3076
  464.2 249.5 %all-gather.9.cloned.1.call-start = ((), (), s32[]{:S(2)}) async-start(), calls=%async_computation.8 | async-start | bytes 9437184 | tf_op jit(solution)/shard_map/all_gather | solution.py:194
  464.7 434.0 %reduce-scatter.9.cloned.1.call-start = ((), (), s32[]{:S(2)}) async-start(), calls=%async_computation.9 | async-start | bytes 9437184 | tf_op jit(solution)/shard_map/reduce_scatter | solution.py:202
  751.4 278.7 %all-gather.11.cloned.1.call-start = ((), (), s32[]{:S(2)}) async-start(), calls=%async_computation.10 | async-start | bytes 9437184 | tf_op jit(solution)/shard_map/all_gather | solution.py:213
  906.0 361.7 %all-reduce.6.cloned.1.call-start = ((), (), s32[]{:S(2)}) async-start(), calls=%async_computation.12 | async-start | bytes 22020096 | tf_op jit(solution)/shard_map/psum | solution.py:245
  906.1 21.9 %slice-start.5 = ((s8[8388608]{0:T(1024)(128)(4,1)}), s8[4194304]{0:T(1024)(128)(4,1)S(1)}, s32[]{:S(2)}) async-start(s8[8388608]{0:T(1024)(128)(4,1)} %bitcast.245), calls=%async_computation.18 | async-start | bytes 8388608
  935.8 100.6 %copy-start.70 = (f32[2,512]{1,0:T(2,128)S(1)}, f32[2,512]{1,0:T(2,128)}, u32[]{:S(2)}) copy-start(f32[2,512]{1,0:T(2,128)} %copy-done.69) | copy-start | bytes 12292
  1071.9 348.6 %reduce-scatter.11.cloned.1.call-start = ((), (), s32[]{:S(2)}) async-start(), calls=%async_computation.11 | async-start | bytes 9437184 | tf_op jit(solution)/shard_map/reduce_scatter | solution.py:231
  1105.4 468.3 %reduce-scatter.7.cloned.1.call-start = ((), (), s32[]{:S(2)}) async-start(), calls=%async_computation.7 | async-start | bytes 9437184 | tf_op jit(solution)/shard_map/reduce_scatter | solution.py:187
  1281.9 138.6 %copy-start.55 = (f32[2048]{0:T(1024)S(1)}, f32[2048]{0:T(1024)}, u32[]{:S(2)}) copy-start(f32[2048]{0:T(1024)} %param.33) | copy-start | bytes 24580
  1281.9 138.6 %copy-start.60 = (f32[256]{0:T(256)S(1)}, f32[256]{0:T(256)}, u32[]{:S(2)}) copy-start(f32[256]{0:T(256)} %copy-done.59) | copy-start | bytes 3076
  1281.9 140.9 %copy-start.56 = (f32[2048]{0:T(1024)S(1)}, f32[2048]{0:T(1024)}, u32[]{:S(2)}) copy-start(f32[2048]{0:T(1024)} %get-tuple-element.123) | copy-start | bytes 24580
  1282.0 291.7 %copy-start.45 = (f32[2048]{0:T(1024)S(1)}, f32[2048]{0:T(1024)}, u32[]{:S(2)}) copy-start(f32[2048]{0:T(1024)} %param.38) | copy-start | bytes 24580
  1282.0 291.7 %copy-start.58 = (f32[256]{0:T(256)S(1)}, f32[256]{0:T(256)}, u32[]{:S(2)}) copy-start(f32[256]{0:T(256)} %copy-done.57) | copy-start | bytes 3076
  1282.0 291.7 %copy-start.62 = (f32[256]{0:T(256)S(1)}, f32[256]{0:T(256)}, u32[]{:S(2)}) copy-start(f32[256]{0:T(256)} %copy-done.61) | copy-start | bytes 3076
  (81 other events, 383.9 us)
Sparse Core Ops, SparseCore 0:
  11.6 127.6 all-gather.4
  178.4 280.9 reduce-scatter.4
  464.3 123.9 all-gather.6
  590.5 123.1 all-gather.8
  751.5 147.1 reduce-scatter.8
  906.1 123.9 all-gather.10
  1072.0 195.5 all-reduce.5
  1271.3 149.1 reduce-scatter.10
  1424.6 149.0 reduce-scatter.6
where the time goes:
time: 1600 us; the launch traced here: 1590 us
  waiting for transfers between devices  1270 us (79%)
  matrix products  205 us (13%)
  other arithmetic  46.1 us (3%)
  blocking collectives  42.8 us (3%)
    reduce_scatter x1, waiting for transfers between devices, body(): lax.psum_scatter(jnp.dot(part_rows, w_out, preferred_element_type=jnp.flo...  281 us
    psum x1, waiting for transfers between devices, body(): lax.psum(grad_query_w.astype(jnp.bfloat16), 'dp').astype(jnp.float32)  151 us
    reduce_scatter x1, waiting for transfers between devices, body(): lax.psum_scatter((times_transposed(grad_gate_act, w_gate) + times_transpo...  147 us
    reduce_scatter x1, waiting for transfers between devices, body(): lax.psum_scatter((times_transposed(grad_query_flat, w_query) + times_tran...  135 us
    all_gather x1, waiting for transfers between devices, body(): gathered_two = lax.all_gather(low_two, 'tensor', axis=0, tiled=True)  124 us
    all_gather x1, waiting for transfers between devices, body(): gathered_one = lax.all_gather(low_one, 'tensor', axis=0, tiled=True)  122 us
    reduce_scatter x1, waiting for transfers between devices, body(): lax.psum_scatter(jnp.dot(part_rows, w_down, preferred_element_type=jnp.fl...  108 us
    all_gather x1, waiting for transfers between devices, body(): grad_rows = lax.all_gather(cotangent, 'tensor', axis=0, tiled=True)  106 us
  transfers between devices with their start and end apart: 9, of which 9 were waited for; matrix products, arithmetic and copies ran while one was open for 7% of the time, Pallas kernels for 0%

commit v1 on v0

--- a/solution.py
+++ b/solution.py
@@ -152,7 +152,23 @@
     doc_row = doc_ids[0]
     inputs = tokens.astype(jnp.float32)
     normed_one, scale_one, low_one = norm_rows(inputs, gain_one)
-    gathered_one = lax.all_gather(low_one, "tensor", axis=0, tiled=True)
+    ways, here, hop = (lax.axis_size("tensor"), lax.axis_index("tensor"), low_one.shape[0])
+    shape = [n * ways if d == 0 else n for d, n in enumerate(low_one.shape)]
+    full = lax.dynamic_update_slice_in_dim(
+        jnp.zeros(shape, low_one.dtype), low_one, here * hop, axis=0
+    )
+    going_up = going_down = low_one
+    for far in range(1, ways // 2 + 1):
+        going_up = lax.ppermute(going_up, "tensor", [(d, (d + 1) % ways) for d in range(ways)])
+        full = lax.dynamic_update_slice_in_dim(full, going_up, (here - far) % ways * hop, axis=0)
+        if 2 * far < ways:
+            going_down = lax.ppermute(
+                going_down, "tensor", [(d, (d - 1) % ways) for d in range(ways)]
+            )
+            full = lax.dynamic_update_slice_in_dim(
+                full, going_down, (here + far) % ways * hop, axis=0
+            )
+    gathered_one = full
     group_rows = gathered_one.shape[0]
     block_rows = min(512, group_rows)
     query_flat = jnp.dot(gathered_one, w_query, preferred_element_type=jnp.float32).astype(

time: 1600 us -> 1650 us (1.031)
  starting transfers between devices: 0.99 us -> 20.5 us
    ppermute x0 -> x7, waiting for transfers between devices: none -> 135 us  [the longest x4 119 us: body(): lax.ppermute(going_up, 'tensor', [(d, (d + 1) % ways) for d in range(ways)])]
    all_gather x1 -> x0, waiting for transfers between devices: 122 us -> none  [body(): gathered_one = lax.all_gather(low_one, 'tensor', axis=0, tiled=True)]
    ppermute x0 -> x7, starting transfers between devices: none -> 19.6 us  [the longest x4 10.4 us: body(): lax.ppermute(going_up, 'tensor', [(d, (d + 1) % ways) for d in range(ways)])]
  transfers between devices with their start and end apart: 9 -> 15, of which waited for: 9 -> 12; matrix products, arithmetic and copies ran while one was open for 7% -> 8% of each run, Pallas kernels for 0% -> 0%
where the time goes in v1:
time: 1650 us
  waiting for transfers between devices  1280 us (78%)
  matrix products  221 us (13%)
  blocking collectives  42.8 us (3%)
  other arithmetic  42.6 us (3%)
  local copies, waits for them, and re-layouts  22.5 us (1%)
  starting transfers between devices  20.5 us (1%)
    reduce_scatter x1, waiting for transfers between devices, body(): lax.psum_scatter(jnp.dot(part_rows, w_out, preferred_element_type=jnp.flo...  280 us
    psum x1, waiting for transfers between devices, body(): lax.psum(grad_query_w.astype(jnp.bfloat16), 'dp').astype(jnp.float32)  151 us
    reduce_scatter x1, waiting for transfers between devices, body(): lax.psum_scatter((times_transposed(grad_gate_act, w_gate) + times_transpo...  147 us
    reduce_scatter x1, waiting for transfers between devices, body(): lax.psum_scatter((times_transposed(grad_query_flat, w_query) + times_tran...  135 us
    all_gather x1, waiting for transfers between devices, body(): gathered_two = lax.all_gather(low_two, 'tensor', axis=0, tiled=True)  123 us
    ppermute x4, waiting for transfers between devices, body(): lax.ppermute(going_up, 'tensor', [(d, (d + 1) % ways) for d in range(ways)])  119 us
    reduce_scatter x1, waiting for transfers between devices, body(): lax.psum_scatter(jnp.dot(part_rows, w_down, preferred_element_type=jnp.fl...  108 us
    all_gather x1, waiting for transfers between devices, body(): grad_rows = lax.all_gather(cotangent, 'tensor', axis=0, tiled=True)  106 us
  transfers between devices with their start and end apart: 15, of which 12 were waited for; matrix products, arithmetic and copies ran while one was open for 8% of the time, Pallas kernels for 0%

profile of v1, /device:TPU:0, one launch (start us, length us, event | category | flops | bytes accessed | tf_op | source)
XLA Modules:
  0.0 1646.0 jit_solution(14260654749032856516)
XLA Ops:
  20.9 42.2 %collective-permute-done = bf16[256,2048]{1,0:T(8,128)(2,1)} collective-permute-done((bf16[256,2048]{1,0:T(8,128)(2,1)}, bf16[256,2048]{1,0:T(8,128)(2,1)}, u32[]{:S(2)}, u32[]{:S(2)}) %collective-permute-start) | collective-permute-done | bytes 1048608 | tf_op jit(solution)/shard_map/ppermute | solution.py:162
  69.8 40.1 %collective-permute-done.2 = bf16[256,2048]{1,0:T(8,128)(2,1)} collective-permute-done((bf16[256,2048]{1,0:T(8,128)(2,1)}, bf16[256,2048]{1,0:T(8,128)(2,1)}, u32[]{:S(2)}, u32[]{:S(2)}) %collective-permute-start.2) | collective-permute-done | bytes 1048608 | tf_op jit(solution)/shard_map/ppermute | solution.py:162
  119.6 36.3 %collective-permute-done.4 = bf16[256,2048]{1,0:T(8,128)(2,1)S(1)} collective-permute-done((bf16[256,2048]{1,0:T(8,128)(2,1)}, bf16[256,2048]{1,0:T(8,128)(2,1)S(1)}, u32[]{:S(2)}, u32[]{:S(2)}) %collective-permute-start.4) | collective-permute-done | bytes 1048608 | tf_op jit(solution)/shard_map/ppermute | solution.py:162
  165.3 16.6 %collective-permute-done.5 = bf16[256,2048]{1,0:T(8,128)(2,1)S(1)} collective-permute-done((bf16[256,2048]{1,0:T(8,128)(2,1)S(1)}, bf16[256,2048]{1,0:T(8,128)(2,1)S(1)}, u32[]{:S(2)}, u32[]{:S(2)}) %collective-permute-start.5) | collective-permute-done | bytes 1048608 | tf_op jit(solution)/shard_map/ppermute | solution.py:165
  222.2 8.2 fusion.82
  230.5 280.2 %reduce-scatter.5.cloned.1.call-done = f32[256,2048]{1,0:T(8,128)} async-done(((f32[2048,2048]{1,0:T(8,128)}), f32[256,2048]{1,0:T(8,128)}) %reduce-scatter.5.cloned.1.call-update) | async-done | bytes 2097168 | tf_op jit(solution)/shard_map/reduce_scatter | solution.py:189
  516.7 123.0 %all-gather.4.cloned.1.call-done = bf16[2048,2048]{1,0:T(8,128)(2,1)} async-done(((bf16[256,2048]{1,0:T(8,128)(2,1)}), bf16[2048,2048]{1,0:T(8,128)(2,1)}) %all-gather.4.cloned.1.call-update) | async-done | bytes 8388624 | tf_op jit(solution)/shard_map/all_gather | solution.py:197
  639.6 11.2 fusion.84
  658.8 106.3 %all-gather.6.cloned.1.call-done = bf16[2048,2048]{1,0:T(8,128)(2,1)} async-done(((bf16[256,2048]{1,0:T(8,128)(2,1)}), bf16[2048,2048]{1,0:T(8,128)(2,1)}) %all-gather.6.cloned.1.call-update) | async-done | bytes 8388624 | tf_op jit(solution)/shard_map/all_gather | solution.py:210
  765.1 14.6 multiply_convert_fusion
  779.8 10.5 fusion.85
  790.3 12.5 add_convert_fusion.1
  802.9 147.3 %reduce-scatter.9.cloned.1.call-done = bf16[256,2048]{1,0:T(8,128)(2,1)} async-done(((bf16[2048,2048]{1,0:T(8,128)(2,1)}), bf16[256,2048]{1,0:T(8,128)(2,1)}) %reduce-scatter.9.cloned.1.call-update) | async-done | bytes 1048592 | tf_op jit(solution)/shard_map/reduce_scatter | solution.py:218
  957.4 10.9 convolution_convert_fusion.1
  968.4 10.9 convolution_convert_fusion.2
  987.1 94.3 %all-gather.8.cloned.1.call-done = bf16[2048,2048]{1,0:T(8,128)(2,1)} async-done(((bf16[256,2048]{1,0:T(8,128)(2,1)}), bf16[2048,2048]{1,0:T(8,128)(2,1)}) %all-gather.8.cloned.1.call-update) | async-done | bytes 8388624 | tf_op jit(solution)/shard_map/all_gather | solution.py:229
  1132.1 8.6 fusion.58
  1140.7 8.1 fusion.86
  1148.8 15.9 add_convert_fusion
  1164.8 11.0 convolution_convert_fusion
  1175.8 151.1 %all-reduce.6.cloned.1.call-done = (bf16[2048,32]{0,1:T(8,128)(2,1)}, bf16[2048,32]{0,1:T(8,128)(2,1)}, bf16[2048,256]{1,0:T(8,128)(2,1)}, bf16[256,2048]{1,0:T(...) async-done(((bf16[2048,32]{0,1:T(8,128)(2,1)}, bf16[2048,32]{0,1:T(8,128)(2,1)}, bf16[2048,256]{1,0:T(8,128)(2,1)}, ...) | async-done | bytes 11010064 | tf_op jit(solution)/shard_map/psum | solution.py:261
  1344.6 135.2 %reduce-scatter.11.cloned.1.call-done = bf16[256,2048]{1,0:T(8,128)(2,1)} async-done(((bf16[2048,2048]{1,0:T(8,128)(2,1)}), bf16[256,2048]{1,0:T(8,128)(2,1)}) %reduce-scatter.11.cloned.1.call-update) | async-done | bytes 1048592 | tf_op jit(solution)/shard_map/reduce_scatter | solution.py:247
  1482.2 42.8 %all-reduce.2 = (f32[2048]{0:T(1024)}, f32[2048]{0:T(1024)}) all-reduce(f32[2048]{0:T(1024)S(1)} %get-tuple-element.125, f32[2048]{0:T(1024)S(1)} %copy-done.57), channel_id=1, replica_groups=mesh['dp'=4,'tensor'=8] {'dp','tensor'}, use_global_device_ids=true, to_apply=%region_17.18 | all-reduce | flops 4096 | bytes 32768 | tf_op jit(solution)/shard_map/psum | solution.py:259
  1525.0 107.9 %reduce-scatter.7.cloned.1.call-done = bf16[256,2048]{1,0:T(8,128)(2,1)} async-done(((bf16[2048,2048]{1,0:T(8,128)(2,1)}), bf16[256,2048]{1,0:T(8,128)(2,1)}) %reduce-scatter.7.cloned.1.call-update) | async-done | bytes 1048592 | tf_op jit(solution)/shard_map/reduce_scatter | solution.py:203
  (304 shorter events, 184.5 us)
Async XLA Ops:
  7.2 758.0 %copy-start = (bf16[704,2048]{1,0:T(8,128)(2,1)S(1)}, bf16[704,2048]{1,0:T(8,128)(2,1)}, u32[]{:S(2)}) copy-start(bf16[704,2048]{1,0:T(8,128)(2,1)} %param.41) | copy-start | bytes 8650756
  7.2 503.5 %reduce-scatter.5.cloned.1.call-start = ((), (), s32[]{:S(2)}) async-start(), calls=%async_computation.4 | async-start | bytes 18874368 | tf_op jit(solution)/shard_map/reduce_scatter | solution.py:189
  15.0 48.2 %collective-permute-start = (bf16[256,2048]{1,0:T(8,128)(2,1)}, bf16[256,2048]{1,0:T(8,128)(2,1)}, u32[]{:S(2)}, u32[]{:S(2)}) collective-permute-start(bf16[256,2048]{1,0:T(8,128)(2,1)} %get-tuple-element.143), channel_id=1, source_target_pairs={{0,1},{1,2},{2,3},{3,4},{4,5},{5,6},{6,7},{7,0},{8,9},{9,10},{10,1... | collective-permute-start | bytes 3145736 | tf_op jit(solution)/shard_map/ppermute | solution.py:162
  17.9 48.6 %collective-permute-start.1 = (bf16[256,2048]{1,0:T(8,128)(2,1)}, bf16[256,2048]{1,0:T(8,128)(2,1)}, u32[]{:S(2)}, u32[]{:S(2)}) collective-permute-start(bf16[256,2048]{1,0:T(8,128)(2,1)} %get-tuple-element.143), channel_id=1, source_target_pairs={{0,7},{1,0},{2,1},{3,2},{4,3},{5,4},{6,5},{7,6},{8,15},{9,8},{10,9... | collective-permute-start | bytes 3145736 | tf_op jit(solution)/shard_map/ppermute | solution.py:165
  63.1 46.8 %collective-permute-start.2 = (bf16[256,2048]{1,0:T(8,128)(2,1)}, bf16[256,2048]{1,0:T(8,128)(2,1)}, u32[]{:S(2)}, u32[]{:S(2)}) collective-permute-start(bf16[256,2048]{1,0:T(8,128)(2,1)} %collective-permute-done), channel_id=1, source_target_pairs={{0,1},{1,2},{2,3},{3,4},{4,5},{5,6},{6,7},{7,0},{8,9},{9,10},{10,1... | collective-permute-start | bytes 3145736 | tf_op jit(solution)/shard_map/ppermute | solution.py:162
  66.5 145.5 %copy-start.19 = (pred[512,1536]{1,0:T(8,128)(4,1)}, pred[512,1536]{1,0:T(8,128)(4,1)S(1)}, u32[]{:S(2)}) copy-start(pred[512,1536]{1,0:T(8,128)(4,1)S(1)} %fusion.10) | copy-start | bytes 2359300
  66.5 47.7 %collective-permute-start.3 = (bf16[256,2048]{1,0:T(8,128)(2,1)}, bf16[256,2048]{1,0:T(8,128)(2,1)S(1)}, u32[]{:S(2)}, u32[]{:S(2)}) collective-permute-start(bf16[256,2048]{1,0:T(8,128)(2,1)} %collective-permute-done.1), channel_id=1, source_target_pairs={{0,7},{1,0},{2,1},{3,2},{4,3},{5,4},{6,5},{7,6},{8,15},{9,8},{10,9... | collective-permute-start | bytes 3145736 | tf_op jit(solution)/shard_map/ppermute | solution.py:165
  109.9 45.9 %collective-permute-start.4 = (bf16[256,2048]{1,0:T(8,128)(2,1)}, bf16[256,2048]{1,0:T(8,128)(2,1)S(1)}, u32[]{:S(2)}, u32[]{:S(2)}) collective-permute-start(bf16[256,2048]{1,0:T(8,128)(2,1)} %collective-permute-done.2), channel_id=1, source_target_pairs={{0,1},{1,2},{2,3},{3,4},{4,5},{5,6},{6,7},{7,0},{8,9},{9,10},{10,1... | collective-permute-start | bytes 3145736 | tf_op jit(solution)/shard_map/ppermute | solution.py:162
  114.2 67.7 %collective-permute-start.5 = (bf16[256,2048]{1,0:T(8,128)(2,1)S(1)}, bf16[256,2048]{1,0:T(8,128)(2,1)S(1)}, u32[]{:S(2)}, u32[]{:S(2)}) collective-permute-start(bf16[256,2048]{1,0:T(8,128)(2,1)S(1)} %collective-permute-done.3), channel_id=1, source_target_pairs={{0,7},{1,0},{2,1},{3,2},{4,3},{5,4},{6,5},{7,6},{8,15},{9,8},{10,9... | collective-permute-start | bytes 3145736 | tf_op jit(solution)/shard_map/ppermute | solution.py:165
  155.9 27.1 %collective-permute-start.6 = (bf16[256,2048]{1,0:T(8,128)(2,1)S(1)}, bf16[256,2048]{1,0:T(8,128)(2,1)S(1)}, u32[]{:S(2)}, u32[]{:S(2)}) collective-permute-start(bf16[256,2048]{1,0:T(8,128)(2,1)S(1)} %collective-permute-done.4), channel_id=1, source_target_pairs={{0,1},{1,2},{2,3},{3,4},{4,5},{5,6},{6,7},{7,0},{8,9},{9,10},{10,1... | collective-permute-start | bytes 3145736 | tf_op jit(solution)/shard_map/ppermute | solution.py:162
  230.5 283.8 %copy-start.44 = (f32[2048]{0:T(1024)S(1)}, f32[2048]{0:T(1024)}, u32[]{:S(2)}) copy-start(f32[2048]{0:T(1024)} %param.38) | copy-start | bytes 24580
  230.5 409.2 %all-gather.4.cloned.1.call-start = ((), (), s32[]{:S(2)}) async-start(), calls=%async_computation.5 | async-start | bytes 9437184 | tf_op jit(solution)/shard_map/all_gather | solution.py:197
  512.9 440.7 %copy-start.58 = (f32[256]{0:T(256)}, f32[256]{0:T(256)S(1)}, u32[]{:S(2)}) copy-start(f32[256]{0:T(256)S(1)} %add_rsqrt_fusion) | copy-start | bytes 3076
  515.5 249.7 %all-gather.6.cloned.1.call-start = ((), (), s32[]{:S(2)}) async-start(), calls=%async_computation.7 | async-start | bytes 9437184 | tf_op jit(solution)/shard_map/all_gather | solution.py:210
  516.2 434.0 %reduce-scatter.9.cloned.1.call-start = ((), (), s32[]{:S(2)}) async-start(), calls=%async_computation.8 | async-start | bytes 9437184 | tf_op jit(solution)/shard_map/reduce_scatter | solution.py:218
  802.9 278.6 %all-gather.8.cloned.1.call-start = ((), (), s32[]{:S(2)}) async-start(), calls=%async_computation.9 | async-start | bytes 9437184 | tf_op jit(solution)/shard_map/all_gather | solution.py:229
  957.4 369.6 %all-reduce.6.cloned.1.call-start = ((), (), s32[]{:S(2)}) async-start(), calls=%async_computation.11 | async-start | bytes 22020096 | tf_op jit(solution)/shard_map/psum | solution.py:261
  1131.3 348.6 %reduce-scatter.11.cloned.1.call-start = ((), (), s32[]{:S(2)}) async-start(), calls=%async_computation.10 | async-start | bytes 9437184 | tf_op jit(solution)/shard_map/reduce_scatter | solution.py:247
  1164.7 468.2 %reduce-scatter.7.cloned.1.call-start = ((), (), s32[]{:S(2)}) async-start(), calls=%async_computation.6 | async-start | bytes 9437184 | tf_op jit(solution)/shard_map/reduce_scatter | solution.py:203
  1341.3 138.6 %copy-start.61 = (f32[256]{0:T(256)S(1)}, f32[256]{0:T(256)}, u32[]{:S(2)}) copy-start(f32[256]{0:T(256)} %copy-done.60) | copy-start | bytes 3076
  1341.3 140.9 %copy-start.57 = (f32[2048]{0:T(1024)S(1)}, f32[2048]{0:T(1024)}, u32[]{:S(2)}) copy-start(f32[2048]{0:T(1024)} %get-tuple-element.123) | copy-start | bytes 24580
  1341.3 291.7 %copy-start.45 = (f32[2048]{0:T(1024)S(1)}, f32[2048]{0:T(1024)}, u32[]{:S(2)}) copy-start(f32[2048]{0:T(1024)} %param.38) | copy-start | bytes 24580
  1341.3 291.7 %copy-start.59 = (f32[256]{0:T(256)S(1)}, f32[256]{0:T(256)}, u32[]{:S(2)}) copy-start(f32[256]{0:T(256)} %copy-done.58) | copy-start | bytes 3076
  1341.3 291.7 %copy-start.63 = (f32[256]{0:T(256)S(1)}, f32[256]{0:T(256)}, u32[]{:S(2)}) copy-start(f32[256]{0:T(256)} %copy-done.62) | copy-start | bytes 3076
  (86 other events, 1227.9 us)
Sparse Core Ops, SparseCore 0:
  230.6 280.0 reduce-scatter.4
  515.6 124.0 all-gather.3
  642.0 123.1 all-gather.5
  803.0 147.1 reduce-scatter.8
  957.5 123.9 all-gather.7
  1131.4 195.5 all-reduce.5
  1330.6 149.1 reduce-scatter.10
  1483.9 149.0 reduce-scatter.6
